TPU v7x, 32 devices: a whole 2x2x4 slice. The times are simulated.
32 devices in a mesh: band: 4 (over x, core), tr: 4 (over z), tc: 2 (over y).
Axes of the slice: x: 2, y: 2, z: 4, core: 2. Of those that a mesh axis runs over, the one named last changes fastest.
Arguments:
- voltages: bfloat16 [4096, 2, 1024], P(('band', 'tr', 'tc')), parts along dimension 0, may hold values from -4 to 4
Outputs:
- visibilities: bfloat16 [128, 2, 1024, 1024], P(('band', 'tc'), None, 'tr'), parts along dimension 0
There are 4 independent parts, one for each index of `band`. A program takes and returns all parts, laid end to end along the dimension named above; each array names one. Nothing has to cross between parts.
All inputs are finite; a program needn't handle non-finite values.
Results may differ from a plain program's by a relative error of at most 0.0054.
Values may be sent and summed in bfloat16 or wider, within the bound.
No kernel may reach another device: no remote copies, remote signals or barrier semaphores. Data moves between devices by JAX's collectives and lax.ppermute only.
A program may use at most 64 MiB of HBM per device.

v0:
```python
import math

import jax
import jax.numpy as jnp
from jax import lax
from jax.sharding import PartitionSpec as P

FINE = 32
TAPS = 16


def shifted(block, axis, distance):
    devices = range(lax.axis_size(axis))
    route = [(i - distance, i) for i in devices if i - distance in devices]
    return lax.ppermute(block, axis, route)


def filter_taps(tap_total, fine_total):
    length = tap_total * fine_total
    position = jnp.arange(length).astype(jnp.float32)
    offset = (position - (length - 1) / 2.0) / fine_total
    prototype = jnp.sin(math.pi * offset) / (math.pi * offset)
    prototype = prototype / jnp.sqrt(jnp.sum(prototype * prototype))
    return prototype.reshape(tap_total, fine_total)


def fourier_table(fine_total):
    indices = jnp.arange(fine_total).astype(jnp.float32)
    angles = 2.0 * math.pi * jnp.mod(indices[:, None] * indices[None, :], fine_total) / fine_total
    cosine = jnp.cos(angles)
    sine_part = jnp.sin(angles)
    stacked = jnp.stack(
        [jnp.stack([cosine, -sine_part], axis=-1), jnp.stack([sine_part, cosine], axis=-1)], axis=1
    )
    return stacked.reshape(2 * fine_total, 2 * fine_total)


def filterbank(extended, hop_count):
    inputs = extended.shape[3]
    tap_table = filter_taps(TAPS, FINE)
    fourier = fourier_table(FINE)
    weighted = jnp.zeros((hop_count, FINE, 2, inputs), jnp.float32)
    for tap_index in range(TAPS):
        weighted = weighted + tap_table[tap_index][None, :, None, None] * extended[
            tap_index : tap_index + hop_count
        ].astype(jnp.float32)
    spectra = jnp.einsum(
        "sjm,jo->som",
        weighted.reshape(hop_count, 2 * FINE, inputs),
        fourier,
        precision=lax.Precision.HIGHEST,
    )
    return spectra.reshape(hop_count, FINE, 2, inputs).astype(jnp.bfloat16)


def per_device(voltages):
    samples = voltages.shape[0]
    inputs = voltages.shape[2]
    hop_count = samples // FINE
    needed = TAPS - 1
    shift_count = (needed + hop_count - 1) // hop_count
    earlier = []
    for distance in range(1, shift_count + 1):
        take_hops = min(hop_count, needed - (distance - 1) * hop_count)
        portion = voltages[samples - take_hops * FINE :]
        arrived = shifted(portion, ("tr", "tc"), distance)
        earlier = [arrived] + earlier
    extended = jnp.concatenate(earlier + [voltages], axis=0).reshape(
        needed + hop_count, FINE, 2, inputs
    )
    spectra = filterbank(extended, hop_count)
    turned = lax.all_to_all(
        lax.all_to_all(spectra, "tr", split_axis=3, concat_axis=0, tiled=True),
        "tc",
        split_axis=1,
        concat_axis=0,
        tiled=True,
    )
    spectra_total = turned.shape[0]
    swapped = jnp.stack([turned[:, :, 1], -turned[:, :, 0]], axis=2)
    stacked = jnp.stack([turned, swapped], axis=0)
    inverse_total = 1.0 / float(spectra_total)
    product = jnp.einsum(
        "rskci,skcj->krij",
        stacked,
        lax.all_gather(turned, "tr", axis=3, tiled=True),
        preferred_element_type=jnp.float32,
    )
    summed = product * inverse_total
    return summed.astype(jnp.bfloat16)


def solution(mesh):
    in_specs = (P(("band", "tr", "tc"), None, None),)
    out_specs = P(("band", "tc"), None, "tr", None)
    return jax.shard_map(
        per_device, mesh=mesh, in_specs=in_specs, out_specs=out_specs, check_vma=False
    )
```

profile of v0, /device:TPU:0, one launch (start us, length us, event | category | flops | bytes accessed | tf_op | source)
XLA Modules:
  0.0 185.9 jit_solution(17419271201619337630)
XLA Ops:
  6.5 0.0 all-gather.2.cloned.1.call-start
  6.5 4.9 %collective-permute-start.3 = (bf16[128,2,1024]{2,1,0:T(2,128)(2,1)}, bf16[128,2,1024]{2,1,0:T(2,128)(2,1)S(1)}, u32[]{:S(2)}, u32[]{:S(2)}) collective-permute-start(bf16[128,2,1024]{2,1,0:T(2,128)(2,1)} %param.1), channel_id=1, source_target_pairs={{0,1},{1,2},{2,3},{3,4},{4,5},{5,6},{6,7},{8,9},{9,10},{10,11},{11... | collective-permute-start | bytes 1572872 | tf_op jit(solution)/shard_map/ppermute | solution.py:15
  11.5 3.5 %collective-permute-start.2 = (bf16[128,2,1024]{2,1,0:T(2,128)(2,1)}, bf16[128,2,1024]{2,1,0:T(2,128)(2,1)S(1)}, u32[]{:S(2)}, u32[]{:S(2)}) collective-permute-start(bf16[128,2,1024]{2,1,0:T(2,128)(2,1)} %param.1), channel_id=1, source_target_pairs={{0,2},{1,3},{2,4},{3,5},{4,6},{5,7},{8,10},{9,11},{10,12},{11,13},... | collective-permute-start | bytes 1572872 | tf_op jit(solution)/shard_map/ppermute | solution.py:15
  15.0 4.4 %collective-permute-start.1 = (bf16[128,2,1024]{2,1,0:T(2,128)(2,1)}, bf16[128,2,1024]{2,1,0:T(2,128)(2,1)S(1)}, u32[]{:S(2)}, u32[]{:S(2)}) collective-permute-start(bf16[128,2,1024]{2,1,0:T(2,128)(2,1)} %param.1), channel_id=1, source_target_pairs={{0,3},{1,4},{2,5},{3,6},{4,7},{8,11},{9,12},{10,13},{11,14},{12,15... | collective-permute-start | bytes 1572872 | tf_op jit(solution)/shard_map/ppermute | solution.py:15
  19.4 1.3 slice.142
  20.7 2.0 %collective-permute-start = (bf16[96,2,1024]{2,1,0:T(2,128)(2,1)S(1)}, bf16[96,2,1024]{2,1,0:T(2,128)(2,1)S(1)}, u32[]{:S(2)}, u32[]{:S(2)}) collective-permute-start(bf16[96,2,1024]{2,1,0:T(2,128)(2,1)S(1)} %slice.142), channel_id=1, source_target_pairs={{0,4},{1,5},{2,6},{3,7},{8,12},{9,13},{10,14},{11,15},{16,20},{17,... | collective-permute-start | bytes 1179656 | tf_op jit(solution)/shard_map/ppermute | solution.py:15
  22.7 0.6 multiply_reduce_fusion
  24.1 0.2 fusion.10
  24.2 0.1 fusion.14
  24.3 0.1 mul.296
  24.4 0.1 mul.356
  24.5 0.1 mul.352
  24.6 0.1 mul.348
  24.7 0.1 mul.344
  24.8 0.1 mul.340
  24.9 0.1 mul.336
  24.9 0.1 mul.332
  25.0 0.1 mul.328
  25.1 0.1 mul.324
  25.2 0.1 mul.320
  25.3 0.1 mul.316
  25.4 0.1 mul.312
  25.5 0.1 mul.308
  25.6 0.1 mul.304
  25.7 0.1 mul.300
  25.8 0.5 copy.16
  26.2 0.6 reshape.353
  26.9 18.9 %collective-permute-done = bf16[96,2,1024]{2,1,0:T(2,128)(2,1)S(1)} collective-permute-done((bf16[96,2,1024]{2,1,0:T(2,128)(2,1)S(1)}, bf16[96,2,1024]{2,1,0:T(2,128)(2,1)S(1)}, u32[]{:S(2)}, u32[]{:S(2)}) %collective-permute-start) | collective-permute-done | bytes 393248 | tf_op jit(solution)/shard_map/ppermute | solution.py:15
  45.7 0.3 constant_dynamic-update-slice_fusion.1
  46.0 0.0 copy-start.1
  46.0 0.0 collective-permute-done.1
  46.0 0.6 constant_dynamic-update-slice_fusion
  46.6 0.0 collective-permute-done.2
  46.6 0.6 constant_dynamic-update-slice_fusion.2
  47.2 0.0 collective-permute-done.3
  47.3 0.6 constant_dynamic-update-slice_fusion.4
  47.9 0.0 copy-done.1
  47.9 0.4 constant_dynamic-update-slice_fusion.6
  48.3 7.2 %multiply_add_fusion = f32[128,2,1024]{2,1,0:T(2,128)S(1)} fusion(bf16[128,2,1024]{2,1,0:T(2,128)(2,1)S(1)} %copy-done.1, bf16[128,2,1024]{2,1,0:T(2,128)(2,1)S(1)} %collective-permute-done.3, bf16[128,2,1024]{2,1,0:T(2,128)(2,1)S(1)} %collective-permute-done.2, bf16[128,2,1024]{2,1,0:T(2,128)(2,1)S(1)} %collective-permute-done.1, f32[128]{0:T(128)S(1)} %mul.356, ...), kind=kLoop, calls=%fused_computation.7 | loop fusion | flops 12320768 | bytes 9445376 | tf_op jit(solution)/shard_map/add | solution.py:44
  55.5 0.7 add.121
  56.2 1.0 fusion.2
  57.3 0.2 convert_element_type.138
  57.5 1.9 %copy.18 = bf16[4,32,2,1024]{1,2,0,3:T(2,128)(2,1)S(1)} copy(bf16[4,32,2,1024]{3,2,1,0:T(2,128)(2,1)S(1)} %convert_element_type.138) | data formatting | bytes 1048576 | tf_op jit(solution)/shard_map/convert_element_type | solution.py:53
  59.4 2.2 %reshape.354 = bf16[4,2,32768]{2,1,0:T(2,128)(2,1)S(1)} reshape(bf16[1024,4,2,32]{3,2,1,0:T(2,128)(2,1)S(1)} %bitcast.32) | data formatting | bytes 1048576
  61.6 39.0 %all_to_all.36 = bf16[4,2,32768]{2,1,0:T(2,128)(2,1)S(1)} all-to-all(bf16[4,2,32768]{2,1,0:T(2,128)(2,1)S(1)} %reshape.354), channel_id=1, replica_groups=mesh['band'=4,'tr'=4,'tc'=2] {'tr'}, dimensions={0} | all-to-all | bytes 1048576 | tf_op jit(solution)/shard_map/all_to_all | solution.py:73
  100.6 1.1 reshape.355
  101.6 2.8 %copy.30 = bf16[4,32,2,4,256]{4,3,1,2,0:T(4,128)(2,1)S(1)} copy(bf16[4,32,2,4,256]{1,2,0,4,3:T(2,128)(2,1)S(1)} %bitcast.33) | data formatting | bytes 1048576 | tf_op jit(solution)/shard_map/all_to_all | solution.py:73
  104.5 0.1 copy.20
  104.6 0.5 copy.21
  105.1 17.1 %all_to_all.37 = bf16[16,32,2,256]{3,2,0,1:T(2,128)(2,1)S(1)} all-to-all(bf16[16,32,2,256]{3,2,0,1:T(2,128)(2,1)S(1)} %copy.21), channel_id=1, replica_groups=mesh['band'=4,'tr'=4,'tc'=2] {'tc'}, dimensions={1} | all-to-all | bytes 1048576 | tf_op jit(solution)/shard_map/all_to_all | solution.py:72
  122.2 0.3 copy.22
  122.5 1.1 copy.23
  123.6 0.0 copy-start
  123.6 0.0 all-gather.2.cloned.1.call-update
  123.7 1.1 fusion.13
  124.8 0.1 maximum_bitcast_fusion
  124.8 44.1 %all-gather.2.cloned.1.call-done = bf16[32,16,2,1024]{3,0,2,1:T(8,128)(2,1)} async-done(((bf16[32,16,2,256]{3,0,2,1:T(8,128)(2,1)}), bf16[32,16,2,1024]{3,0,2,1:T(8,128)(2,1)}) %all-gather.2.cloned.1.call-update) | async-done | bytes 2097168 | tf_op jit(solution)/shard_map/all_gather | solution.py:86
  168.9 0.0 copy-done
  168.9 10.1 %fusion = bf16[16,2,256,1024]{3,2,1,0:T(8,128)(2,1)} fusion(bf16[32,16,2,1024]{3,0,2,1:T(8,128)(2,1)} %all-gather.2.cloned.1.call-done, bf16[1,32,16,2,256]{4,1,3,2,0:T(8,128)(2,1)S(1)} %maximum_bitcast_fusion, bf16[1,32,16,2,256]{4,1,3,2,0:T(8,128)(2,1)S(1)} %bitcast.36), kind=kOutput, calls=%fused_computation.1 | convolution fusion | flops 1091043328 | bytes 19922944 | tf_op jit(solution)/shard_map/rskci,skcj->krij/dot_general | solution.py:83
  (20 shorter events, 0.1 us)
Async XLA Ops:
  6.5 162.4 %all-gather.2.cloned.1.call-start = ((), (), s32[]{:S(2)}) async-start(), calls=%async_computation.2 | async-start | bytes 2621440 | tf_op jit(solution)/shard_map/all_gather | solution.py:86
  6.5 40.7 %collective-permute-start.3 = (bf16[128,2,1024]{2,1,0:T(2,128)(2,1)}, bf16[128,2,1024]{2,1,0:T(2,128)(2,1)S(1)}, u32[]{:S(2)}, u32[]{:S(2)}) collective-permute-start(bf16[128,2,1024]{2,1,0:T(2,128)(2,1)} %param.1), channel_id=1, source_target_pairs={{0,1},{1,2},{2,3},{3,4},{4,5},{5,6},{6,7},{8,9},{9,10},{10,11},{11... | collective-permute-start | bytes 1572872 | tf_op jit(solution)/shard_map/ppermute | solution.py:15
  11.5 35.2 %collective-permute-start.2 = (bf16[128,2,1024]{2,1,0:T(2,128)(2,1)}, bf16[128,2,1024]{2,1,0:T(2,128)(2,1)S(1)}, u32[]{:S(2)}, u32[]{:S(2)}) collective-permute-start(bf16[128,2,1024]{2,1,0:T(2,128)(2,1)} %param.1), channel_id=1, source_target_pairs={{0,2},{1,3},{2,4},{3,5},{4,6},{5,7},{8,10},{9,11},{10,12},{11,13},... | collective-permute-start | bytes 1572872 | tf_op jit(solution)/shard_map/ppermute | solution.py:15
  15.0 31.1 %collective-permute-start.1 = (bf16[128,2,1024]{2,1,0:T(2,128)(2,1)}, bf16[128,2,1024]{2,1,0:T(2,128)(2,1)S(1)}, u32[]{:S(2)}, u32[]{:S(2)}) collective-permute-start(bf16[128,2,1024]{2,1,0:T(2,128)(2,1)} %param.1), channel_id=1, source_target_pairs={{0,3},{1,4},{2,5},{3,6},{4,7},{8,11},{9,12},{10,13},{11,14},{12,15... | collective-permute-start | bytes 1572872 | tf_op jit(solution)/shard_map/ppermute | solution.py:15
  20.7 25.0 %collective-permute-start = (bf16[96,2,1024]{2,1,0:T(2,128)(2,1)S(1)}, bf16[96,2,1024]{2,1,0:T(2,128)(2,1)S(1)}, u32[]{:S(2)}, u32[]{:S(2)}) collective-permute-start(bf16[96,2,1024]{2,1,0:T(2,128)(2,1)S(1)} %slice.142), channel_id=1, source_target_pairs={{0,4},{1,5},{2,6},{3,7},{8,12},{9,13},{10,14},{11,15},{16,20},{17,... | collective-permute-start | bytes 1179656 | tf_op jit(solution)/shard_map/ppermute | solution.py:15
  46.0 1.9 copy-start.1
  123.6 45.3 %copy-start = (bf16[2,16,16,2,256]{4,1,0,3,2:T(8,128)(2,1)S(1)}, bf16[2,16,16,2,256]{4,1,0,3,2:T(8,128)(2,1)}, u32[]{:S(2)}) copy-start(bf16[2,16,16,2,256]{4,1,0,3,2:T(8,128)(2,1)} %copy.23) | copy-start | bytes 1572868
Sparse Core Ops, SparseCore 0:
  123.8 45.1 all-gather.1
where the time goes:
time: 186 us
  waiting for transfers between devices  63 us (34%)
  blocking collectives  56.1 us (30%)
  local copies, waits for them, and re-layouts  17.3 us (9%)
  starting transfers between devices  14.8 us (8%)
  between operations  14.3 us (8%)
  matrix products  11.2 us (6%)
  other arithmetic  9.29 us (5%)
    all_gather x1, waiting for transfers between devices, per_device(): lax.all_gather(turned, 'tr', axis=3, tiled=True)  44.1 us
    all_to_all x1, blocking collectives, per_device(): lax.all_to_all(spectra, 'tr', split_axis=3, concat_axis=0, tiled=True)  39 us
    ppermute x4, waiting for transfers between devices, shifted(): return lax.ppermute(block, axis, route)  18.9 us
    all_to_all x1, blocking collectives, per_device(): lax.all_to_all(lax.all_to_all(spectra, 'tr', split_axis=3, concat_axis=0,...  17.1 us
    ppermute x4, starting transfers between devices, shifted(): return lax.ppermute(block, axis, route)  14.8 us
    dot_general x1, matrix products, per_device(): jnp.einsum('rskci,skcj->krij', stacked, lax.all_gather(turned, 'tr', axis...  10.1 us
    add x1, other arithmetic, filterbank(): weighted + tap_table[tap_index][None, :, None, None] * extended[tap_index...  7.23 us
  transfers between devices with their start and end apart: 5, of which 2 were waited for; matrix products, arithmetic and copies ran while one was open for 4% of the time, Pallas kernels for 0%

commit v1 on v0

--- a/solution.py
+++ b/solution.py
@@ -2,7 +2,10 @@
 
 import jax
 import jax.numpy as jnp
+import numpy as np
 from jax import lax
+from jax.experimental import pallas as pl
+from jax.experimental.pallas import tpu as pltpu
 from jax.sharding import PartitionSpec as P
 
 FINE = 32
@@ -53,7 +56,7 @@
     return spectra.reshape(hop_count, FINE, 2, inputs).astype(jnp.bfloat16)
 
 
-def per_device(voltages):
+def streamed(voltages):
     samples = voltages.shape[0]
     inputs = voltages.shape[2]
     hop_count = samples // FINE
@@ -90,9 +93,154 @@
     return summed.astype(jnp.bfloat16)
 
 
+def stacked_operator(hops):
+    position = np.arange(TAPS * FINE, dtype=np.float64)
+    offset = (position - (TAPS * FINE - 1) / 2.0) / FINE
+    prototype = np.sinc(offset)
+    taps = (prototype / np.sqrt(np.sum(prototype * prototype))).reshape(TAPS, FINE)
+    indices = np.arange(FINE)
+    angles = 2.0 * np.pi * np.mod(np.outer(indices, indices), FINE) / FINE
+    cosine, sine = np.cos(angles), np.sin(angles)
+    fourier = np.stack([np.stack([cosine, -sine], -1), np.stack([sine, cosine], -1)], 1)
+    reach = (TAPS - 2 + hops) // hops + 1
+    matrix = np.zeros((reach, FINE, 2, hops, hops, FINE, 2))
+    for distance in range(reach):
+        for out_hop in range(hops):
+            for in_hop in range(hops):
+                tap = in_hop - out_hop + TAPS - 1 - hops * distance
+                if 0 <= tap < TAPS:
+                    weighted = taps[tap][:, None, None, None] * fourier
+                    matrix[distance, :, :, out_hop, in_hop] = weighted.transpose(2, 3, 0, 1)
+    return matrix.reshape(reach, FINE, 2 * hops, hops * FINE * 2)
+
+
+def split_in_two(matrix):
+    high = matrix.astype(np.float32).astype(jnp.bfloat16)
+    low = (matrix - high.astype(np.float64)).astype(np.float32).astype(jnp.bfloat16)
+    return high, low
+
+
+def correlate(blocks, places, valid, operator, row_block, blocks_total, rows_total):
+    wide, inputs = blocks[0].shape
+    reach_rows = operator.shape[1]
+    channels = operator.shape[3]
+    count = len(blocks)
+    per_block = operator.shape[4]
+    step_rows = channels * per_block
+    half = per_block // 2
+    spectra_total = blocks_total * half
+    scale = 1.0 / float(spectra_total)
+
+    def kernel(info, operator_ref, *refs):
+        block_refs, out_ref, sums = refs[:count], refs[count], refs[count + 1]
+        channel = pl.program_id(0)
+
+        @pl.when(channel == 0)
+        def _():
+            sums[...] = jnp.zeros_like(sums)
+            high = operator_ref[0].reshape(reach_rows * step_rows, wide)
+            low = operator_ref[1].reshape(reach_rows * step_rows, wide)
+            for b in range(count):
+
+                @pl.when(info[count + b] == 1)
+                def _(b=b):
+                    block = block_refs[b][...]
+                    start = pl.multiple_of(info[b] * step_rows, step_rows)
+                    where = pl.ds(start, reach_rows * step_rows)
+                    sums[where, :] += jnp.dot(
+                        high, block, preferred_element_type=jnp.float32
+                    ) + jnp.dot(low, block, preferred_element_type=jnp.float32)
+
+        first = pl.multiple_of(info[2 * count] * rows_total, rows_total)
+        everything, rows, turned = [], [], []
+        sign = jnp.where(
+            lax.broadcasted_iota(jnp.int32, (per_block, rows_total), 0) < half, 1.0, -1.0
+        )
+        for s in range(blocks_total):
+            place = pl.multiple_of(s * step_rows + channel * per_block, per_block)
+            everything.append(sums[pl.ds(place, per_block), :])
+            mine = sums[pl.ds(place, per_block), pl.ds(first, rows_total)]
+            rows.append(mine)
+            turned.append(pltpu.roll(mine, half, 0) * sign)
+        right = jnp.concatenate(everything, 0).astype(jnp.bfloat16)
+        for part, pieces in enumerate((rows, turned)):
+            left = jnp.concatenate(pieces, 0).astype(jnp.bfloat16)
+            product = lax.dot_general(
+                left, right, (((0,), (0,)), ((), ())), preferred_element_type=jnp.float32
+            )
+            out_ref[0, part] = (product * scale).astype(jnp.bfloat16)
+
+    info = jnp.stack(
+        [jnp.asarray(v, jnp.int32) for v in (*places, *valid, row_block[0], row_block[1])]
+    )
+    at = 2 * count + 1
+    return pl.pallas_call(
+        kernel,
+        grid_spec=pltpu.PrefetchScalarGridSpec(
+            num_scalar_prefetch=1,
+            grid=(channels,),
+            in_specs=[
+                pl.BlockSpec(
+                    (2, reach_rows, None, channels, per_block, wide),
+                    lambda k, info: (0, 0, info[at], 0, 0, 0),
+                )
+            ]
+            + [pl.BlockSpec((wide, inputs), lambda k, info: (0, 0))] * count,
+            out_specs=pl.BlockSpec((1, 2, rows_total, inputs), lambda k, info: (k, 0, 0, 0)),
+            scratch_shapes=[
+                pltpu.VMEM(((blocks_total + reach_rows - 1) * step_rows, inputs), jnp.float32)
+            ],
+        ),
+        out_shape=jax.ShapeDtypeStruct((channels, 2, rows_total, inputs), jnp.bfloat16),
+        compiler_params=pltpu.CompilerParams(vmem_limit_bytes=48 * 2**20),
+        name="filter_and_correlate",
+    )(info, operator, *blocks)
+
+
+def gathered(voltages):
+    samples, _, inputs = voltages.shape
+    hops = samples // FINE
+    line, pair = lax.axis_size("tr"), lax.axis_size("tc")
+    here, side = lax.axis_index("tr"), lax.axis_index("tc")
+    own = voltages.reshape(samples * 2, inputs)
+
+    def across(block):
+        return lax.ppermute(block, "tc", [(0, 1), (1, 0)])
+
+    far = lax.ppermute(own, "tr", [(i, i ^ 2) for i in range(line)])
+    up = lax.ppermute(own, "tr", [(0, 1), (1, 2), (2, 3)])
+    down = lax.ppermute(own, "tr", [(1, 0), (2, 1), (3, 2)])
+    end = lax.ppermute(far, "tr", [(2, 3), (1, 0)])
+    lines = [
+        (own, here, 1),
+        (up, here - 1, here > 0),
+        (down, here + 1, here < line - 1),
+        (far, here ^ 2, 1),
+        (end, line - 1 - here, (here == 0) | (here == line - 1)),
+    ]
+    blocks, places, valid = [], [], []
+    for block, place, ok in lines:
+        for array, which in ((block, side), (across(block), 1 - side)):
+            blocks.append(array)
+            places.append(jnp.clip(place, 0, line - 1) * pair + which)
+            valid.append(ok)
+    matrix = stacked_operator(hops)
+    reach = matrix.shape[0]
+    matrix = matrix.reshape(reach, pair, FINE // pair, 2 * hops, samples * 2)
+    operator = jnp.asarray(np.stack(split_in_two(matrix)))
+    return correlate(
+        blocks, places, valid, operator, (here, side), line * pair, inputs // line
+    )
+
+
 def solution(mesh):
     in_specs = (P(("band", "tr", "tc"), None, None),)
     out_specs = P(("band", "tc"), None, "tr", None)
+    small = mesh.shape["tr"] == 4 and mesh.shape["tc"] == 2
     return jax.shard_map(
-        per_device, mesh=mesh, in_specs=in_specs, out_specs=out_specs, check_vma=False
-    )
+        gathered if small else streamed,
+        mesh=mesh,
+        in_specs=in_specs,
+        out_specs=out_specs,
+        check_vma=False,
+    )

time: 186 us -> 111 us (0.60)
  blocking collectives: 56.1 us -> 0 us
  Pallas kernels: 0 us -> 21.5 us
  local copies, waits for them, and re-layouts: 17.3 us -> 1.33 us
  between operations: 14.3 us -> 0.04 us
  matrix products: 11.2 us -> 0 us
  other arithmetic: 9.29 us -> 0 us
  waiting for transfers between devices: 63 us -> 70 us
  starting transfers between devices: 14.8 us -> 16.7 us
    all_to_all x2 -> x0, blocking collectives: 56.1 us -> none  [the longest x1 39 us: per_device(): lax.all_to_all(spectra, 'tr', split_axis=3, concat_axis=0, tiled=True)]
    ppermute x4 -> x9, waiting for transfers between devices: 18.9 us -> 70 us  [the longest x5 43.1 us: across(): return lax.ppermute(block, 'tc', [(0, 1), (1, 0)])]
    all_gather x1 -> x0, waiting for transfers between devices: 44.1 us -> none  [per_device(): lax.all_gather(turned, 'tr', axis=3, tiled=True)]
    pallas_call x0 -> x1, Pallas kernels: none -> 21.5 us  [correlate(): pl.pallas_call(kernel, grid_spec=pltpu.PrefetchScalarGridSpec(num_scalar_...]
    dot_general x2 -> x0, matrix products: 11.2 us -> none  [the longest x1 10.1 us: per_device(): jnp.einsum('rskci,skcj->krij', stacked, lax.all_gather(turned, 'tr', axis...]
    add x1 -> x0, other arithmetic: 7.23 us -> none  [filterbank(): weighted + tap_table[tap_index][None, :, None, None] * extended[tap_index...]
    all_to_all x5 -> x0, local copies, waits for them, and re-layouts: 4.82 us -> none  [the longest x3 3.45 us: per_device(): lax.all_to_all(spectra, 'tr', split_axis=3, concat_axis=0, tiled=True)]
    unnamed x7 -> x0, local copies, waits for them, and re-layouts: 3.53 us -> none
  transfers between devices with their start and end apart: 5 -> 9, of which waited for: 2 -> 7; matrix products, arithmetic and copies ran while one was open for 4% -> 0% of each run, Pallas kernels for 0% -> 0%
where the time goes in v1:
time: 111 us; the launch traced here: 110 us
  waiting for transfers between devices  70 us (63%)
  Pallas kernels  21.5 us (19%)
  starting transfers between devices  16.7 us (15%)
  local copies, waits for them, and re-layouts  1.33 us (1%)
    ppermute x5, waiting for transfers between devices, across(): return lax.ppermute(block, 'tc', [(0, 1), (1, 0)])  43.1 us
    pallas_call x1, Pallas kernels, correlate(): pl.pallas_call(kernel, grid_spec=pltpu.PrefetchScalarGridSpec(num_scalar_...  21.5 us
    ppermute x1, waiting for transfers between devices, gathered(): far = lax.ppermute(own, 'tr', [(i, i ^ 2) for i in range(line)])  18.2 us
    ppermute x1, waiting for transfers between devices, gathered(): end = lax.ppermute(far, 'tr', [(2, 3), (1, 0)])  8.7 us
    ppermute x5, starting transfers between devices, across(): return lax.ppermute(block, 'tc', [(0, 1), (1, 0)])  5.43 us
    ppermute x1, starting transfers between devices, gathered(): up = lax.ppermute(own, 'tr', [(0, 1), (1, 2), (2, 3)])  4.58 us
    ppermute x1, starting transfers between devices, gathered(): far = lax.ppermute(own, 'tr', [(i, i ^ 2) for i in range(line)])  4.13 us
  transfers between devices with their start and end apart: 9, of which 7 were waited for; matrix products, arithmetic and copies ran while one was open for 0% of the time, Pallas kernels for 0%

profile of v1, /device:TPU:0, one launch (start us, length us, event | category | flops | bytes accessed | tf_op | source)
XLA Modules:
  0.0 109.6 jit_solution(6037400620438615091)
XLA Ops:
  0.0 1.2 %reshape.3.refs_0_ = bf16[256,1024]{1,0:T(8,128)(2,1)S(1)} reshape(bf16[128,2,1024]{2,1,0:T(2,128)(2,1)} %param.2) | data formatting | bytes 1048576 | tf_op jit(solution)/shard_map/reshape | solution.py:205
  1.2 4.1 %collective-permute-start.5 = (bf16[256,1024]{1,0:T(8,128)(2,1)S(1)}, bf16[256,1024]{1,0:T(8,128)(2,1)S(1)}, u32[]{:S(2)}, u32[]{:S(2)}) collective-permute-start(bf16[256,1024]{1,0:T(8,128)(2,1)S(1)} %reshape.3.refs_0_), channel_id=1, source_target_pairs={{0,4},{2,6},{4,0},{6,2},{1,5},{3,7},{5,1},{7,3},{8,12},{10,14},{12... | collective-permute-start | bytes 1572872 | tf_op jit(solution)/shard_map/ppermute | solution.py:210
  5.4 1.3 %collective-permute-start.3 = (bf16[256,1024]{1,0:T(8,128)(2,1)S(1)}, bf16[256,1024]{1,0:T(8,128)(2,1)S(1)}, u32[]{:S(2)}, u32[]{:S(2)}) collective-permute-start(bf16[256,1024]{1,0:T(8,128)(2,1)S(1)} %reshape.3.refs_0_), channel_id=1, source_target_pairs={{2,0},{4,2},{6,4},{3,1},{5,3},{7,5},{10,8},{12,10},{14,12},{11,9},... | collective-permute-start | bytes 1572872 | tf_op jit(solution)/shard_map/ppermute | solution.py:212
  6.7 4.6 %collective-permute-start.1 = (bf16[256,1024]{1,0:T(8,128)(2,1)S(1)}, bf16[256,1024]{1,0:T(8,128)(2,1)S(1)}, u32[]{:S(2)}, u32[]{:S(2)}) collective-permute-start(bf16[256,1024]{1,0:T(8,128)(2,1)S(1)} %reshape.3.refs_0_), channel_id=1, source_target_pairs={{0,2},{2,4},{4,6},{1,3},{3,5},{5,7},{8,10},{10,12},{12,14},{9,11},... | collective-permute-start | bytes 1572872 | tf_op jit(solution)/shard_map/ppermute | solution.py:211
  11.2 18.2 %collective-permute-done.5.refs_6_ = bf16[256,1024]{1,0:T(8,128)(2,1)S(1)} collective-permute-done((bf16[256,1024]{1,0:T(8,128)(2,1)S(1)}, bf16[256,1024]{1,0:T(8,128)(2,1)S(1)}, u32[]{:S(2)}, u32[]{:S(2)}) %collective-permute-start.5) | collective-permute-done | bytes 524320 | tf_op jit(solution)/shard_map/ppermute | solution.py:210
  29.4 1.3 %collective-permute-start.7 = (bf16[256,1024]{1,0:T(8,128)(2,1)S(1)}, bf16[256,1024]{1,0:T(8,128)(2,1)S(1)}, u32[]{:S(2)}, u32[]{:S(2)}) collective-permute-start(bf16[256,1024]{1,0:T(8,128)(2,1)S(1)} %collective-permute-done.5.refs_6_), channel_id=1, source_target_pairs={{4,6},{2,0},{5,7},{3,1},{12,14},{10,8},{13,15},{11,9},{20,22},{18,... | collective-permute-start | bytes 1572872 | tf_op jit(solution)/shard_map/ppermute | solution.py:213
  30.7 1.9 %collective-permute-start = (bf16[256,1024]{1,0:T(8,128)(2,1)S(1)}, bf16[256,1024]{1,0:T(8,128)(2,1)S(1)}, u32[]{:S(2)}, u32[]{:S(2)}) collective-permute-start(bf16[256,1024]{1,0:T(8,128)(2,1)S(1)} %reshape.3.refs_0_), channel_id=1, source_target_pairs={{0,1},{1,0},{2,3},{3,2},{4,5},{5,4},{6,7},{7,6},{8,9},{9,8},{10,11... | collective-permute-start | bytes 1572872 | tf_op jit(solution)/shard_map/ppermute | solution.py:208
  32.6 0.2 collective-permute-start.6
  32.8 0.0 collective-permute-done.3.refs_4_
  32.8 1.8 %collective-permute-start.4 = (bf16[256,1024]{1,0:T(8,128)(2,1)S(1)}, bf16[256,1024]{1,0:T(8,128)(2,1)}, u32[]{:S(2)}, u32[]{:S(2)}) collective-permute-start(bf16[256,1024]{1,0:T(8,128)(2,1)S(1)} %collective-permute-done.3.refs_4_), channel_id=1, source_target_pairs={{0,1},{1,0},{2,3},{3,2},{4,5},{5,4},{6,7},{7,6},{8,9},{9,8},{10,11... | collective-permute-start | bytes 1572872 | tf_op jit(solution)/shard_map/ppermute | solution.py:208
  34.6 0.0 collective-permute-done.1.refs_2_
  34.6 0.2 collective-permute-start.2
  34.8 8.7 %collective-permute-done.7.refs_8_ = bf16[256,1024]{1,0:T(8,128)(2,1)S(1)} collective-permute-done((bf16[256,1024]{1,0:T(8,128)(2,1)S(1)}, bf16[256,1024]{1,0:T(8,128)(2,1)S(1)}, u32[]{:S(2)}, u32[]{:S(2)}) %collective-permute-start.7) | collective-permute-done | bytes 524320 | tf_op jit(solution)/shard_map/ppermute | solution.py:213
  43.5 1.3 %collective-permute-start.8 = (bf16[256,1024]{1,0:T(8,128)(2,1)S(1)}, bf16[256,1024]{1,0:T(8,128)(2,1)}, u32[]{:S(2)}, u32[]{:S(2)}) collective-permute-start(bf16[256,1024]{1,0:T(8,128)(2,1)S(1)} %collective-permute-done.7.refs_8_), channel_id=1, source_target_pairs={{0,1},{1,0},{2,3},{3,2},{4,5},{5,4},{6,7},{7,6},{8,9},{9,8},{10,11... | collective-permute-start | bytes 1572872 | tf_op jit(solution)/shard_map/ppermute | solution.py:208
  44.9 0.1 stack.78.info
  45.0 0.6 collective-permute-done.refs_1_
  45.6 11.3 %collective-permute-done.6.refs_7_ = bf16[256,1024]{1,0:T(8,128)(2,1)} collective-permute-done((bf16[256,1024]{1,0:T(8,128)(2,1)S(1)}, bf16[256,1024]{1,0:T(8,128)(2,1)}, u32[]{:S(2)}, u32[]{:S(2)}) %collective-permute-start.6) | collective-permute-done | bytes 524320 | tf_op jit(solution)/shard_map/ppermute | solution.py:208
  56.9 11.2 %collective-permute-done.4.refs_5_ = bf16[256,1024]{1,0:T(8,128)(2,1)} collective-permute-done((bf16[256,1024]{1,0:T(8,128)(2,1)S(1)}, bf16[256,1024]{1,0:T(8,128)(2,1)}, u32[]{:S(2)}, u32[]{:S(2)}) %collective-permute-start.4) | collective-permute-done | bytes 524320 | tf_op jit(solution)/shard_map/ppermute | solution.py:208
  68.2 11.2 %collective-permute-done.2.refs_3_ = bf16[256,1024]{1,0:T(8,128)(2,1)} collective-permute-done((bf16[256,1024]{1,0:T(8,128)(2,1)S(1)}, bf16[256,1024]{1,0:T(8,128)(2,1)}, u32[]{:S(2)}, u32[]{:S(2)}) %collective-permute-start.2) | collective-permute-done | bytes 524320 | tf_op jit(solution)/shard_map/ppermute | solution.py:208
  79.4 8.7 %collective-permute-done.8.refs_9_ = bf16[256,1024]{1,0:T(8,128)(2,1)} collective-permute-done((bf16[256,1024]{1,0:T(8,128)(2,1)S(1)}, bf16[256,1024]{1,0:T(8,128)(2,1)}, u32[]{:S(2)}, u32[]{:S(2)}) %collective-permute-start.8) | collective-permute-done | bytes 524320 | tf_op jit(solution)/shard_map/ppermute | solution.py:208
  88.1 21.5 %filter_and_correlate.1 = bf16[16,2,256,1024]{3,2,1,0:T(8,128)(2,1)} custom-call(s32[22]{0:T(128)S(1)} %stack.78.info, bf16[2,5,2,16,8,256]{5,4,3,2,1,0:T(8,128)(2,1)} %constant.21.clone.operator_ref, bf16[256,1024]{1,0:T(8,128)(2,1)S(1)} %reshape.3.refs_0_, bf16[256,1024]{1,0:T(8,128)(2,1)S(1)} %collective-permute-done.refs_1_, ...), custom_call_target="tpu_custom_call" | custom-call | tf_op jit(solution)/shard_map/filter_and_correlate/pallas_call | solution.py:177
  (1 shorter events, 0.0 us)
Async XLA Ops:
  1.2 28.2 %collective-permute-start.5 = (bf16[256,1024]{1,0:T(8,128)(2,1)S(1)}, bf16[256,1024]{1,0:T(8,128)(2,1)S(1)}, u32[]{:S(2)}, u32[]{:S(2)}) collective-permute-start(bf16[256,1024]{1,0:T(8,128)(2,1)S(1)} %reshape.3.refs_0_), channel_id=1, source_target_pairs={{0,4},{2,6},{4,0},{6,2},{1,5},{3,7},{5,1},{7,3},{8,12},{10,14},{12... | collective-permute-start | bytes 1572872 | tf_op jit(solution)/shard_map/ppermute | solution.py:210
  5.4 27.4 %collective-permute-start.3 = (bf16[256,1024]{1,0:T(8,128)(2,1)S(1)}, bf16[256,1024]{1,0:T(8,128)(2,1)S(1)}, u32[]{:S(2)}, u32[]{:S(2)}) collective-permute-start(bf16[256,1024]{1,0:T(8,128)(2,1)S(1)} %reshape.3.refs_0_), channel_id=1, source_target_pairs={{2,0},{4,2},{6,4},{3,1},{5,3},{7,5},{10,8},{12,10},{14,12},{11,9},... | collective-permute-start | bytes 1572872 | tf_op jit(solution)/shard_map/ppermute | solution.py:212
  6.7 28.0 %collective-permute-start.1 = (bf16[256,1024]{1,0:T(8,128)(2,1)S(1)}, bf16[256,1024]{1,0:T(8,128)(2,1)S(1)}, u32[]{:S(2)}, u32[]{:S(2)}) collective-permute-start(bf16[256,1024]{1,0:T(8,128)(2,1)S(1)} %reshape.3.refs_0_), channel_id=1, source_target_pairs={{0,2},{2,4},{4,6},{1,3},{3,5},{5,7},{8,10},{10,12},{12,14},{9,11},... | collective-permute-start | bytes 1572872 | tf_op jit(solution)/shard_map/ppermute | solution.py:211
  29.4 14.1 %collective-permute-start.7 = (bf16[256,1024]{1,0:T(8,128)(2,1)S(1)}, bf16[256,1024]{1,0:T(8,128)(2,1)S(1)}, u32[]{:S(2)}, u32[]{:S(2)}) collective-permute-start(bf16[256,1024]{1,0:T(8,128)(2,1)S(1)} %collective-permute-done.5.refs_6_), channel_id=1, source_target_pairs={{4,6},{2,0},{5,7},{3,1},{12,14},{10,8},{13,15},{11,9},{20,22},{18,... | collective-permute-start | bytes 1572872 | tf_op jit(solution)/shard_map/ppermute | solution.py:213
  30.7 14.9 %collective-permute-start = (bf16[256,1024]{1,0:T(8,128)(2,1)S(1)}, bf16[256,1024]{1,0:T(8,128)(2,1)S(1)}, u32[]{:S(2)}, u32[]{:S(2)}) collective-permute-start(bf16[256,1024]{1,0:T(8,128)(2,1)S(1)} %reshape.3.refs_0_), channel_id=1, source_target_pairs={{0,1},{1,0},{2,3},{3,2},{4,5},{5,4},{6,7},{7,6},{8,9},{9,8},{10,11... | collective-permute-start | bytes 1572872 | tf_op jit(solution)/shard_map/ppermute | solution.py:208
  32.6 24.3 %collective-permute-start.6 = (bf16[256,1024]{1,0:T(8,128)(2,1)S(1)}, bf16[256,1024]{1,0:T(8,128)(2,1)}, u32[]{:S(2)}, u32[]{:S(2)}) collective-permute-start(bf16[256,1024]{1,0:T(8,128)(2,1)S(1)} %collective-permute-done.5.refs_6_), channel_id=1, source_target_pairs={{0,1},{1,0},{2,3},{3,2},{4,5},{5,4},{6,7},{7,6},{8,9},{9,8},{10,11... | collective-permute-start | bytes 1572872 | tf_op jit(solution)/shard_map/ppermute | solution.py:208
  32.8 35.3 %collective-permute-start.4 = (bf16[256,1024]{1,0:T(8,128)(2,1)S(1)}, bf16[256,1024]{1,0:T(8,128)(2,1)}, u32[]{:S(2)}, u32[]{:S(2)}) collective-permute-start(bf16[256,1024]{1,0:T(8,128)(2,1)S(1)} %collective-permute-done.3.refs_4_), channel_id=1, source_target_pairs={{0,1},{1,0},{2,3},{3,2},{4,5},{5,4},{6,7},{7,6},{8,9},{9,8},{10,11... | collective-permute-start | bytes 1572872 | tf_op jit(solution)/shard_map/ppermute | solution.py:208
  34.6 44.7 %collective-permute-start.2 = (bf16[256,1024]{1,0:T(8,128)(2,1)S(1)}, bf16[256,1024]{1,0:T(8,128)(2,1)}, u32[]{:S(2)}, u32[]{:S(2)}) collective-permute-start(bf16[256,1024]{1,0:T(8,128)(2,1)S(1)} %collective-permute-done.1.refs_2_), channel_id=1, source_target_pairs={{0,1},{1,0},{2,3},{3,2},{4,5},{5,4},{6,7},{7,6},{8,9},{9,8},{10,11... | collective-permute-start | bytes 1572872 | tf_op jit(solution)/shard_map/ppermute | solution.py:208
  43.5 44.5 %collective-permute-start.8 = (bf16[256,1024]{1,0:T(8,128)(2,1)S(1)}, bf16[256,1024]{1,0:T(8,128)(2,1)}, u32[]{:S(2)}, u32[]{:S(2)}) collective-permute-start(bf16[256,1024]{1,0:T(8,128)(2,1)S(1)} %collective-permute-done.7.refs_8_), channel_id=1, source_target_pairs={{0,1},{1,0},{2,3},{3,2},{4,5},{5,4},{6,7},{7,6},{8,9},{9,8},{10,11... | collective-permute-start | bytes 1572872 | tf_op jit(solution)/shard_map/ppermute | solution.py:208
